TPU v7x, 32 devices: a whole 2x2x4 slice. The times are simulated.
32 devices in a mesh: member: 4 (over x, core), space: 8 (over z, y).
Axes of the slice: x: 2, y: 2, z: 4, core: 2. Of those that a mesh axis runs over, the one named last changes fastest.
Arguments:
- features: bfloat16 [4, 641, 192, 128], P('member', None, 'space'), may hold values from -6 to 6
- depth_kernel: float32 [641, 5, 5], replicated, may hold values from -1.25 to 1.25
- in_weight: bfloat16 [641, 1282], replicated, may hold values from -0.25 to 0.25
- out_weight: bfloat16 [1282, 641], replicated, may hold values from -0.15625 to 0.15625
- decoder_weight: bfloat16 [641, 72], replicated, may hold values from -0.25 to 0.25
- observed: float32 [72, 192, 128], P(None, 'space'), may hold values from -6 to 6
- land_mask: int32 [192, 128], P('space'), may hold values 0 or 1
Outputs:
- grad_features: bfloat16 [4, 641, 192, 128], P('member', None, 'space')
- decoder_grad: float32 [641, 72], replicated
All inputs are finite; a program needn't handle non-finite values. No bound on the sum of `land_mask` on one device may be relied on, other than what follows from the above.
Results may differ from a plain program's by a relative error of at most 0.0054.
Values may be sent and summed in bfloat16 or wider, within the bound.
A program may use at most 128 MiB of HBM per device.

v0:
```python
import math
import jax
import jax.numpy as jnp
from jax import lax
from jax.sharding import PartitionSpec as P

norm_eps = 1e-05


def padded_2(cells, sides, width):
    for axis, dim in sides:
        count = lax.axis_size(axis)
        head = lax.slice_in_dim(cells, 0, width, axis=dim)
        tail = lax.slice_in_dim(cells, cells.shape[dim] - width, cells.shape[dim], axis=dim)
        cells = jnp.concatenate(
            [
                lax.ppermute(tail, axis, [(i, (i + 1) % count) for i in range(count)]),
                cells,
                lax.ppermute(head, axis, [((i + 1) % count, i) for i in range(count)]),
            ],
            axis=dim,
        )
    return cells


def per_device(features, depth_kernel, in_weight, out_weight, decoder_weight, observed, land_mask):
    channels = features.shape[1]
    lon_len = features.shape[2]
    lat_len = features.shape[3]
    points = lon_len * lat_len
    padded = padded_2(features, (("space", 2),), 2)
    widened = jnp.pad(padded.astype(jnp.float32), ((0, 0), (0, 0), (0, 0), (2, 2)))
    convolved = jnp.zeros(features.shape, jnp.float32)
    for row_off in range(5):
        for col_off in range(5):
            convolved = (
                convolved
                + depth_kernel[:, row_off, col_off][None, :, None, None]
                * widened[:, :, row_off : row_off + lon_len, col_off : col_off + lat_len]
            )
    center = jnp.mean(convolved, axis=1, keepdims=True)
    shifted = convolved - center
    normed = (
        shifted * lax.rsqrt(jnp.mean(shifted * shifted, axis=1, keepdims=True) + norm_eps)
    ).astype(jnp.bfloat16)
    flat = normed.reshape(channels, points)
    hidden = jax.nn.gelu(
        jnp.einsum("ch,cp->hp", in_weight, flat, preferred_element_type=jnp.float32),
        approximate=False,
    ).astype(jnp.bfloat16)
    mlp_out = jnp.einsum("hc,hp->cp", out_weight, hidden, preferred_element_type=jnp.float32)
    block_out = (features.reshape(channels, points).astype(jnp.float32) + mlp_out).astype(
        jnp.bfloat16
    )
    decoded_flat = jnp.einsum(
        "co,cp->op", decoder_weight, block_out, preferred_element_type=jnp.float32
    ).astype(jnp.bfloat16)
    outputs = decoded_flat.shape[0]
    decoded = decoded_flat.reshape(1, outputs, lon_len, lat_len)
    groups = lax.axis_size("member")
    members = features.shape[0] * groups
    point_weight = 4.0 + 8.0 * land_mask.astype(jnp.float32)
    own_f = decoded.astype(jnp.float32)
    apart = own_f - lax.all_gather(decoded, "member", axis=0, tiled=True).astype(jnp.float32)
    apart_norm = jnp.sqrt(jnp.sum(apart * apart, axis=1, keepdims=True) + 1.0)
    pair_sum = jnp.sum(apart / apart_norm, axis=0, keepdims=True)
    misfit = own_f - observed[None]
    misfit_norm = jnp.sqrt(jnp.sum(misfit * misfit, axis=1, keepdims=True) + 1.0)
    score_grad = (point_weight[None, None] * (misfit / misfit_norm - pair_sum / members)).astype(
        jnp.bfloat16
    )
    grad_flat = score_grad.reshape(outputs, points)
    grad_features = jnp.einsum(
        "co,op->cp", decoder_weight, grad_flat, preferred_element_type=jnp.float32
    ).astype(jnp.bfloat16)
    total_points = lon_len * lax.axis_size("space") * lat_len
    term = jnp.einsum(
        "cp,op->co", block_out, grad_flat, preferred_element_type=jnp.float32
    ) / math.sqrt(members * total_points)
    decoder_grad = lax.psum(term, ("member", "space"))
    return (grad_features.reshape(features.shape), decoder_grad)


def solution(mesh):
    placed = (
        P("member", None, "space", None),
        P(),
        P(),
        P(),
        P(),
        P(None, "space", None),
        P("space", None),
    )
    return jax.shard_map(
        per_device,
        mesh=mesh,
        in_specs=placed,
        out_specs=(P("member", None, "space", None), P()),
        check_vma=False,
    )
```

profile of v0, /device:TPU:8, one launch (start us, length us, event | category | flops | bytes accessed | tf_op | source)
XLA Modules:
  0.0 393.1 jit_solution(12034791294327075821)
XLA Ops:
  7.2 0.0 copy-start
  7.2 0.0 all-gather.2.cloned.1.call-start
  7.2 2.3 fusion.106
  9.6 1.6 collective-permute-start
  11.3 1.5 collective-permute-start.1
  12.7 2.6 convert_bitcast_fusion
  15.3 0.5 pad.8
  15.9 0.0 copy-start.8
  15.9 0.0 copy-start.5
  15.9 5.0 %copy.15 = f32[81,8,24,128]{3,1,2,0:T(8,128)} copy(f32[81,8,24,128]{3,2,1,0:T(8,128)S(1)} %bitcast.131) | data formatting | bytes 15925248
  20.9 0.1 slice_reduce_fusion.23
  21.0 0.2 slice_reduce_fusion.24
  21.1 4.2 %collective-permute-done = bf16[1,641,2,128]{3,1,2,0:T(8,128)(2,1)S(1)} collective-permute-done((bf16[1,641,2,128]{3,1,2,0:T(8,128)(2,1)S(1)}, bf16[1,641,2,128]{3,1,2,0:T(8,128)(2,1)S(1)}, u32[]{:S(2)}, u32[]{:S(2)}) %collective-permute-start) | collective-permute-done | bytes 328224 | tf_op jit(solution)/shard_map/ppermute | solution.py:17
  25.4 0.3 copy.11
  25.6 1.6 collective-permute-done.1
  27.2 0.3 copy.12
  27.5 6.9 %maximum_convert_fusion = f32[1,641,28,128]{3,2,1,0:T(8,128)} fusion(bf16[1,641,2,128]{3,2,1,0:T(2,128)(2,1)S(1)} %copy.12, bf16[1,641,24,128]{3,2,1,0:T(8,128)(2,1)S(1)} %copy-done.5, bf16[1,641,2,128]{3,2,1,0:T(2,128)(2,1)S(1)} %copy.11), kind=kLoop, calls=%fused_computation.100 | loop fusion | flops 13784064 | bytes 13784064 | tf_op jit(solution)/shard_map/convert_element_type | solution.py:32
  34.4 130.6 %fusion.104 = (f32[24,128]{1,0:T(8,128)S(1)}, f32[1,641,24,128]{3,2,1,0:T(8,128)}) fusion(f32[641]{0:T(1024)S(1)} %get-tuple-element.25, f32[641]{0:T(1024)S(1)} %get-tuple-element.26, f32[1,641,28,128]{3,2,1,0:T(8,128)} %maximum_convert_fusion, f32[641]{0:T(1024)S(1)} %get-tuple-element.3, f32[641]{0:T(1024)S(1)} %get-tuple-element.4, ...), kind=kLoop, calls=%fused_computation.177 | loop fusion | flops 98454528 | bytes 57838180 | tf_op jit(solution)/shard_map/reduce_sum | solution.py:41
  165.0 4.3 %multiply_reduce_fusion = f32[24,128]{1,0:T(8,128)S(1)} fusion(f32[1,641,24,128]{3,2,1,0:T(8,128)} %get-tuple-element.28, f32[24,128]{1,0:T(8,128)S(1)} %broadcast_multiply_fusion), kind=kLoop, calls=%fused_computation.99 | loop fusion | flops 5904384 | bytes 7901184 | tf_op jit(solution)/shard_map/reduce_sum | solution.py:44
  169.3 1.1 copy-done.2
  170.4 0.9 fusion.69
  171.3 0.7 pad.9
  172.0 0.0 slice-start
  172.0 1.1 copy.16
  173.2 0.0 copy-start.10
  173.2 42.9 %fusion.123 = bf16[1282,3072]{1,0:T(8,128)(2,1)S(1)} fusion(bf16[641,3072]{1,0:T(8,128)(2,1)S(1)} %bitcast.142, bf16[641,1282]{1,0:T(8,128)(2,1)S(1)} %copy-done), kind=kOutput, calls=%fused_computation.23.clone.clone.clone.clone.1 | convolution fusion | flops 5304895488 | bytes 13458436 | tf_op jit(solution)/shard_map/ch,cp->hp/dot_general | solution.py:48
  216.1 0.0 copy-start.7
  216.2 7.2 %fusion.18 = bf16[641,3072]{1,0:T(8,128)(2,1)S(1)} fusion(f32[641,3072]{1,0:T(8,128)S(1)} %bitcast.138, bf16[1282,641]{0,1:T(8,128)(2,1)S(1)} %copy-done.10, bf16[1282,3072]{1,0:T(8,128)(2,1)S(1)} %fusion.123), kind=kOutput, calls=%fused_computation.45 | convolution fusion | flops 5052844032 | bytes 21335044 | tf_op jit(solution)/shard_map/hc,hp->cp/dot_general | solution.py:51
  223.4 1.9 copy-done.3
  225.3 0.8 convolution_convert_fusion.1
  226.1 0.8 copy.18
  226.9 0.0 all-gather.2.cloned.1.call-update
  226.9 0.0 all-reduce.3.cloned.1.call-start
  227.0 0.1 convert_bitcast_fusion.1
  227.1 0.2 copy.17
  227.2 0.2 multiply_reduce_fusion.2
  227.4 20.9 %all-gather.2.cloned.1.call-done = bf16[4,72,24,128]{3,2,1,0:T(8,128)(2,1)} async-done(((bf16[1,72,24,128]{3,2,1,0:T(8,128)(2,1)}), bf16[4,72,24,128]{3,2,1,0:T(8,128)(2,1)}) %all-gather.2.cloned.1.call-update) | async-done | bytes 1769488 | tf_op jit(solution)/shard_map/all_gather | solution.py:64
  248.4 2.1 multiply_reduce_fusion.1
  250.5 2.0 divide_reduce_fusion
  252.5 0.2 multiply_convert_fusion.1
  252.7 2.0 convolution_multiply_fusion
  254.7 3.1 convolution_convert_fusion
  257.9 0.0 all-reduce.3.cloned.1.call-update
  257.9 0.0 copy-start.1
  257.9 3.4 copy.20
  261.3 2.6 slice_bitcast_fusion
  263.9 120.7 %all-reduce.3.cloned.1.call-done = f32[641,72]{0,1:T(8,128)} async-done(((f32[641,72]{0,1:T(8,128)}), f32[641,72]{0,1:T(8,128)}) %all-reduce.3.cloned.1.call-update) | async-done | bytes 184624 | tf_op jit(solution)/shard_map/psum | solution.py:80
  384.6 1.6 copy.30
  (24 shorter events, 0.2 us)
Async XLA Ops:
  7.2 166.0 %copy-start = (bf16[641,1282]{1,0:T(8,128)(2,1)S(1)}, bf16[641,1282]{1,0:T(8,128)(2,1)}, u32[]{:S(2)}) copy-start(bf16[641,1282]{1,0:T(8,128)(2,1)} %param.9) | copy-start | bytes 4930576
  7.2 241.2 %all-gather.2.cloned.1.call-start = ((), (), s32[]{:S(2)}) async-start(), calls=%async_computation | async-start | bytes 2211840 | tf_op jit(solution)/shard_map/all_gather | solution.py:64
  9.6 15.7 %collective-permute-start = (bf16[1,641,2,128]{3,1,2,0:T(8,128)(2,1)S(1)}, bf16[1,641,2,128]{3,1,2,0:T(8,128)(2,1)S(1)}, u32[]{:S(2)}, u32[]{:S(2)}) collective-permute-start(bf16[1,641,2,128]{3,1,2,0:T(8,128)(2,1)S(1)} %copy.13), channel_id=1, source_target_pairs={{0,1},{1,2},{2,3},{3,4},{4,5},{5,6},{6,7},{7,0},{8,9},{9,10},{10,1... | collective-permute-start | bytes 984584 | tf_op jit(solution)/shard_map/ppermute | solution.py:17
  11.3 16.0 %collective-permute-start.1 = (bf16[1,641,2,128]{3,1,2,0:T(8,128)(2,1)S(1)}, bf16[1,641,2,128]{3,1,2,0:T(8,128)(2,1)S(1)}, u32[]{:S(2)}, u32[]{:S(2)}) collective-permute-start(bf16[1,641,2,128]{3,1,2,0:T(8,128)(2,1)S(1)} %copy.14), channel_id=1, source_target_pairs={{1,0},{2,1},{3,2},{4,3},{5,4},{6,5},{7,6},{0,7},{9,8},{10,9},{11,1... | collective-permute-start | bytes 984584 | tf_op jit(solution)/shard_map/ppermute | solution.py:19
  15.9 5.0 %copy-start.8 = (f32[641,5,5]{0,2,1:T(8,128)S(1)}, f32[641,5,5]{0,2,1:T(8,128)}, u32[]{:S(2)}) copy-start(f32[641,5,5]{0,2,1:T(8,128)} %param.8) | copy-start | bytes 192304
  15.9 11.6 %copy-start.5 = (bf16[1,641,24,128]{3,2,1,0:T(8,128)(2,1)S(1)}, bf16[1,641,24,128]{3,2,1,0:T(8,128)(2,1)}, u32[]{:S(2)}) copy-start(bf16[1,641,24,128]{3,2,1,0:T(8,128)(2,1)} %param.7) | copy-start | bytes 11814916
  164.9 5.5 %copy-start.2 = (f32[1,641,24,128]{3,2,1,0:T(8,128)S(1)}, f32[1,641,24,128]{3,2,1,0:T(8,128)}, u32[]{:S(2)}) copy-start(f32[1,641,24,128]{3,2,1,0:T(8,128)} %get-tuple-element.28) | copy-start | bytes 23629828
  172.0 44.1 %slice-start = ((s8[7962624]{0:T(1024)(128)(4,1)}), s8[4194304]{0:T(1024)(128)(4,1)S(1)}, s32[]{:S(2)}) async-start(s8[7962624]{0:T(1024)(128)(4,1)} %bitcast.136), calls=%async_computation.2 | async-start | bytes 8388608
  173.1 43.0 %slice-start.1 = ((s8[7962624]{0:T(1024)(128)(4,1)}), s8[3768320]{0:T(1024)(128)(4,1)S(1)}, s32[]{:S(2)}) async-start(s8[7962624]{0:T(1024)(128)(4,1)} %bitcast.136), calls=%async_computation.3 | async-start | bytes 7536640
  173.2 43.0 %copy-start.10 = (bf16[1282,641]{0,1:T(8,128)(2,1)S(1)}, bf16[1282,641]{0,1:T(8,128)(2,1)}, u32[]{:S(2)}) copy-start(bf16[1282,641]{0,1:T(8,128)(2,1)} %param.10) | copy-start | bytes 4930576
  216.1 9.1 %copy-start.7 = (bf16[641,72]{0,1:T(8,128)(2,1)S(1)}, bf16[641,72]{0,1:T(8,128)(2,1)}, u32[]{:S(2)}) copy-start(bf16[641,72]{0,1:T(8,128)(2,1)} %param.11) | copy-start | bytes 276916
  223.4 1.9 copy-start.3
  225.3 1.9 copy-start.6
  225.3 2.1 copy-start.9
  226.9 157.7 %all-reduce.3.cloned.1.call-start = ((), (), s32[]{:S(2)}) async-start(), calls=%async_computation.1 | async-start | bytes 442368 | tf_op jit(solution)/shard_map/psum | solution.py:80
  248.3 4.4 %copy-start.4 = (bf16[641,3072]{1,0:T(8,128)(2,1)S(1)}, bf16[641,3072]{1,0:T(8,128)(2,1)}, u32[]{:S(2)}) copy-start(bf16[641,3072]{1,0:T(8,128)(2,1)} %copy-done.3) | copy-start | bytes 11814916
  257.9 128.3 %copy-start.1 = (bf16[641,1282]{1,0:T(8,128)(2,1)S(1)}, bf16[641,1282]{1,0:T(8,128)(2,1)}, u32[]{:S(2)}) copy-start(bf16[641,1282]{1,0:T(8,128)(2,1)} %param.9) | copy-start | bytes 4930576
Sparse Core Ops, SparseCore 0:
  227.0 21.2 all-gather.1
  258.0 126.5 all-reduce.2
where the time goes:
time: 393 us
  other arithmetic  150 us (38%)
  waiting for transfers between devices  148 us (38%)
  matrix products  56.1 us (14%)
  local copies, waits for them, and re-layouts  22.2 us (6%)
  between operations  14.3 us (4%)
    reduce_sum x1, other arithmetic, per_device(): center = jnp.mean(convolved, axis=1, keepdims=True)  131 us
    psum x1, waiting for transfers between devices, per_device(): decoder_grad = lax.psum(term, ('member', 'space'))  121 us
    dot_general x1, matrix products, per_device(): jnp.einsum('ch,cp->hp', in_weight, flat, preferred_element_type=jnp.float32)  42.9 us
    all_gather x1, waiting for transfers between devices, per_device(): lax.all_gather(decoded, 'member', axis=0, tiled=True).astype(jnp.float32)  20.9 us
    unnamed x36, local copies, waits for them, and re-layouts  16.6 us
  transfers between devices with their start and end apart: 4, of which 4 were waited for; matrix products, arithmetic and copies ran while one was open for 4% of the time, Pallas kernels for 0%

commit v1 on v0

--- a/solution.py
+++ b/solution.py
@@ -77,7 +77,9 @@
     term = jnp.einsum(
         "cp,op->co", block_out, grad_flat, preferred_element_type=jnp.float32
     ) / math.sqrt(members * total_points)
-    decoder_grad = lax.psum(term, ("member", "space"))
+    decoder_grad = term
+    for over in ("space", "member"):
+        decoder_grad = lax.psum(decoder_grad, over)
     return (grad_features.reshape(features.shape), decoder_grad)
 
 

time: 393 us -> 369 us (0.939)
  waiting for transfers between devices: 148 us -> 122 us
    psum x1 -> x2, waiting for transfers between devices: 121 us -> 95.5 us  [per_device(): decoder_grad = lax.psum(decoder_grad, over)]
  transfers between devices with their start and end apart: 4 -> 5, of which waited for: 4 -> 5; matrix products, arithmetic and copies ran while one was open for 4% -> 5% of each run, Pallas kernels for 0% -> 0%
where the time goes in v1:
time: 369 us; the launch traced here: 368 us
  other arithmetic  150 us (41%)
  waiting for transfers between devices  122 us (33%)
  matrix products  54.2 us (15%)
  local copies, waits for them, and re-layouts  24 us (7%)
  between operations  14 us (4%)
    reduce_sum x1, other arithmetic, per_device(): center = jnp.mean(convolved, axis=1, keepdims=True)  131 us
    psum x2, waiting for transfers between devices, per_device(): decoder_grad = lax.psum(decoder_grad, over)  95.5 us
    dot_general x1, matrix products, per_device(): jnp.einsum('ch,cp->hp', in_weight, flat, preferred_element_type=jnp.float32)  42.9 us
    all_gather x1, waiting for transfers between devices, per_device(): lax.all_gather(decoded, 'member', axis=0, tiled=True).astype(jnp.float32)  20.9 us
    unnamed x36, local copies, waits for them, and re-layouts  16.2 us
  transfers between devices with their start and end apart: 5, of which 5 were waited for; matrix products, arithmetic and copies ran while one was open for 5% of the time, Pallas kernels for 0%

profile of v1, /device:TPU:8, one launch (start us, length us, event | category | flops | bytes accessed | tf_op | source)
XLA Modules:
  0.0 367.5 jit_solution(1414615255015293656)
XLA Ops:
  7.2 0.0 copy-start
  7.2 0.0 all-gather.2.cloned.1.call-start
  7.2 2.3 fusion.106
  9.6 1.6 collective-permute-start
  11.3 1.5 collective-permute-start.1
  12.7 2.6 convert_bitcast_fusion
  15.3 0.5 pad.8
  15.9 0.0 copy-start.5
  15.9 5.0 %copy.15 = f32[81,8,24,128]{3,1,2,0:T(8,128)} copy(f32[81,8,24,128]{3,2,1,0:T(8,128)S(1)} %bitcast.131) | data formatting | bytes 15925248
  20.9 0.1 slice_reduce_fusion.23
  21.0 0.2 slice_reduce_fusion.24
  21.1 4.2 %collective-permute-done = bf16[1,641,2,128]{3,1,2,0:T(8,128)(2,1)S(1)} collective-permute-done((bf16[1,641,2,128]{3,1,2,0:T(8,128)(2,1)S(1)}, bf16[1,641,2,128]{3,1,2,0:T(8,128)(2,1)S(1)}, u32[]{:S(2)}, u32[]{:S(2)}) %collective-permute-start) | collective-permute-done | bytes 328224 | tf_op jit(solution)/shard_map/ppermute | solution.py:17
  25.4 0.3 copy.11
  25.6 1.6 collective-permute-done.1
  27.2 0.3 copy.12
  27.5 6.9 %maximum_convert_fusion = f32[1,641,28,128]{3,2,1,0:T(8,128)} fusion(bf16[1,641,2,128]{3,2,1,0:T(2,128)(2,1)S(1)} %copy.12, bf16[1,641,24,128]{3,2,1,0:T(8,128)(2,1)S(1)} %copy-done.5, bf16[1,641,2,128]{3,2,1,0:T(2,128)(2,1)S(1)} %copy.11), kind=kLoop, calls=%fused_computation.100 | loop fusion | flops 13784064 | bytes 13784064 | tf_op jit(solution)/shard_map/convert_element_type | solution.py:32
  34.4 130.5 %fusion.104 = (f32[24,128]{1,0:T(8,128)S(1)}, f32[1,641,24,128]{3,2,1,0:T(8,128)}) fusion(f32[641]{0:T(1024)S(1)} %get-tuple-element.25, f32[641]{0:T(1024)S(1)} %get-tuple-element.26, f32[1,641,28,128]{3,2,1,0:T(8,128)} %maximum_convert_fusion, f32[641]{0:T(1024)S(1)} %get-tuple-element.3, f32[641]{0:T(1024)S(1)} %get-tuple-element.4, ...), kind=kLoop, calls=%fused_computation.177 | loop fusion | flops 98454528 | bytes 57838180 | tf_op jit(solution)/shard_map/reduce_sum | solution.py:41
  164.9 4.3 %multiply_reduce_fusion = f32[24,128]{1,0:T(8,128)S(1)} fusion(f32[1,641,24,128]{3,2,1,0:T(8,128)} %get-tuple-element.28, f32[24,128]{1,0:T(8,128)S(1)} %broadcast_multiply_fusion), kind=kLoop, calls=%fused_computation.99 | loop fusion | flops 5904384 | bytes 7901184 | tf_op jit(solution)/shard_map/reduce_sum | solution.py:44
  169.2 1.1 copy-done.2
  170.4 0.9 fusion.69
  171.2 0.7 pad.9
  171.9 1.1 copy.16
  173.1 0.0 copy-start.10
  173.1 42.9 %fusion.123 = bf16[1282,3072]{1,0:T(8,128)(2,1)S(1)} fusion(bf16[641,3072]{1,0:T(8,128)(2,1)S(1)} %bitcast.142, bf16[641,1282]{1,0:T(8,128)(2,1)S(1)} %copy-done), kind=kOutput, calls=%fused_computation.23.clone.clone.clone.clone.1 | convolution fusion | flops 5304895488 | bytes 13458436 | tf_op jit(solution)/shard_map/ch,cp->hp/dot_general | solution.py:48
  216.1 7.2 %fusion.18 = bf16[641,3072]{1,0:T(8,128)(2,1)S(1)} fusion(f32[641,3072]{1,0:T(8,128)S(1)} %bitcast.138, bf16[1282,641]{0,1:T(8,128)(2,1)S(1)} %copy-done.10, bf16[1282,3072]{1,0:T(8,128)(2,1)S(1)} %fusion.123), kind=kOutput, calls=%fused_computation.45 | convolution fusion | flops 5052844032 | bytes 21335044 | tf_op jit(solution)/shard_map/hc,hp->cp/dot_general | solution.py:51
  223.4 1.9 copy-done.3
  225.2 0.8 convolution_convert_fusion.1
  226.0 0.8 copy.18
  226.9 0.0 all-gather.2.cloned.1.call-update
  226.9 0.0 all-reduce.4.cloned.1.call-start
  226.9 0.1 convert_bitcast_fusion.1
  227.0 0.2 copy.17
  227.2 0.2 multiply_reduce_fusion.2
  227.4 20.9 %all-gather.2.cloned.1.call-done = bf16[4,72,24,128]{3,2,1,0:T(8,128)(2,1)} async-done(((bf16[1,72,24,128]{3,2,1,0:T(8,128)(2,1)}), bf16[4,72,24,128]{3,2,1,0:T(8,128)(2,1)}) %all-gather.2.cloned.1.call-update) | async-done | bytes 1769488 | tf_op jit(solution)/shard_map/all_gather | solution.py:64
  248.3 2.1 multiply_reduce_fusion.1
  250.4 2.0 divide_reduce_fusion
  252.5 0.2 multiply_convert_fusion.1
  252.7 2.0 convolution_multiply_fusion
  254.7 0.0 all-reduce.4.cloned.1.call-update
  254.7 0.0 all-reduce.6.cloned.1.call-start
  254.8 1.2 convolution_convert_fusion
  256.0 0.0 copy-start.1
  256.0 3.0 copy.20
  259.1 66.1 %all-reduce.4.cloned.1.call-done = f32[641,72]{0,1:T(8,128)} async-done(((f32[641,72]{0,1:T(8,128)}), f32[641,72]{0,1:T(8,128)}) %all-reduce.4.cloned.1.call-update) | async-done | bytes 184624 | tf_op jit(solution)/shard_map/psum | solution.py:82
  325.2 0.0 all-reduce.6.cloned.1.call-update
  325.2 4.7 %slice_bitcast_fusion = bf16[1,641,24,128]{3,2,1,0:T(8,128)(2,1)} fusion(bf16[648,24,128]{2,1,0:T(8,128)(2,1)} %bitcast.135), kind=kLoop, calls=%fused_computation.103 | loop fusion | bytes 7876608 | tf_op jit(solution)/shard_map/reshape | solution.py:83
  329.9 29.4 %all-reduce.6.cloned.1.call-done = f32[641,72]{0,1:T(8,128)} async-done(((f32[641,72]{0,1:T(8,128)}), f32[641,72]{0,1:T(8,128)}) %all-reduce.6.cloned.1.call-update) | async-done | bytes 184624 | tf_op jit(solution)/shard_map/psum | solution.py:82
  359.3 1.6 copy.31
  (27 shorter events, 0.2 us)
Async XLA Ops:
  7.2 165.9 %copy-start = (bf16[641,1282]{1,0:T(8,128)(2,1)S(1)}, bf16[641,1282]{1,0:T(8,128)(2,1)}, u32[]{:S(2)}) copy-start(bf16[641,1282]{1,0:T(8,128)(2,1)} %param.9) | copy-start | bytes 4930576
  7.2 241.1 %all-gather.2.cloned.1.call-start = ((), (), s32[]{:S(2)}) async-start(), calls=%async_computation | async-start | bytes 2211840 | tf_op jit(solution)/shard_map/all_gather | solution.py:64
  9.6 15.7 %collective-permute-start = (bf16[1,641,2,128]{3,1,2,0:T(8,128)(2,1)S(1)}, bf16[1,641,2,128]{3,1,2,0:T(8,128)(2,1)S(1)}, u32[]{:S(2)}, u32[]{:S(2)}) collective-permute-start(bf16[1,641,2,128]{3,1,2,0:T(8,128)(2,1)S(1)} %copy.13), channel_id=1, source_target_pairs={{0,1},{1,2},{2,3},{3,4},{4,5},{5,6},{6,7},{7,0},{8,9},{9,10},{10,1... | collective-permute-start | bytes 984584 | tf_op jit(solution)/shard_map/ppermute | solution.py:17
  11.3 16.0 %collective-permute-start.1 = (bf16[1,641,2,128]{3,1,2,0:T(8,128)(2,1)S(1)}, bf16[1,641,2,128]{3,1,2,0:T(8,128)(2,1)S(1)}, u32[]{:S(2)}, u32[]{:S(2)}) collective-permute-start(bf16[1,641,2,128]{3,1,2,0:T(8,128)(2,1)S(1)} %copy.14), channel_id=1, source_target_pairs={{1,0},{2,1},{3,2},{4,3},{5,4},{6,5},{7,6},{0,7},{9,8},{10,9},{11,1... | collective-permute-start | bytes 984584 | tf_op jit(solution)/shard_map/ppermute | solution.py:19
  15.9 5.0 %copy-start.8 = (f32[641,5,5]{0,2,1:T(8,128)S(1)}, f32[641,5,5]{0,2,1:T(8,128)}, u32[]{:S(2)}) copy-start(f32[641,5,5]{0,2,1:T(8,128)} %param.8) | copy-start | bytes 192304
  15.9 11.6 %copy-start.5 = (bf16[1,641,24,128]{3,2,1,0:T(8,128)(2,1)S(1)}, bf16[1,641,24,128]{3,2,1,0:T(8,128)(2,1)}, u32[]{:S(2)}) copy-start(bf16[1,641,24,128]{3,2,1,0:T(8,128)(2,1)} %param.7) | copy-start | bytes 11814916
  164.9 5.5 %copy-start.2 = (f32[1,641,24,128]{3,2,1,0:T(8,128)S(1)}, f32[1,641,24,128]{3,2,1,0:T(8,128)}, u32[]{:S(2)}) copy-start(f32[1,641,24,128]{3,2,1,0:T(8,128)} %get-tuple-element.28) | copy-start | bytes 23629828
  171.9 44.1 %slice-start = ((s8[7962624]{0:T(1024)(128)(4,1)}), s8[4194304]{0:T(1024)(128)(4,1)S(1)}, s32[]{:S(2)}) async-start(s8[7962624]{0:T(1024)(128)(4,1)} %bitcast.136), calls=%async_computation.3 | async-start | bytes 8388608
  173.1 43.0 %slice-start.1 = ((s8[7962624]{0:T(1024)(128)(4,1)}), s8[3768320]{0:T(1024)(128)(4,1)S(1)}, s32[]{:S(2)}) async-start(s8[7962624]{0:T(1024)(128)(4,1)} %bitcast.136), calls=%async_computation.4 | async-start | bytes 7536640
  173.1 43.0 %copy-start.10 = (bf16[1282,641]{0,1:T(8,128)(2,1)S(1)}, bf16[1282,641]{0,1:T(8,128)(2,1)}, u32[]{:S(2)}) copy-start(bf16[1282,641]{0,1:T(8,128)(2,1)} %param.10) | copy-start | bytes 4930576
  216.1 9.1 %copy-start.7 = (bf16[641,72]{0,1:T(8,128)(2,1)S(1)}, bf16[641,72]{0,1:T(8,128)(2,1)}, u32[]{:S(2)}) copy-start(bf16[641,72]{0,1:T(8,128)(2,1)} %param.11) | copy-start | bytes 276916
  223.4 1.9 copy-start.3
  225.2 1.9 copy-start.6
  225.2 2.1 copy-start.9
  226.9 98.3 %all-reduce.4.cloned.1.call-start = ((), (), s32[]{:S(2)}) async-start(), calls=%async_computation.1 | async-start | bytes 442368 | tf_op jit(solution)/shard_map/psum | solution.py:82
  248.3 4.4 %copy-start.4 = (bf16[641,3072]{1,0:T(8,128)(2,1)S(1)}, bf16[641,3072]{1,0:T(8,128)(2,1)}, u32[]{:S(2)}) copy-start(bf16[641,3072]{1,0:T(8,128)(2,1)} %copy-done.3) | copy-start | bytes 11814916
  254.7 104.6 %all-reduce.6.cloned.1.call-start = ((), (), s32[]{:S(2)}) async-start(), calls=%async_computation.2 | async-start | bytes 442368 | tf_op jit(solution)/shard_map/psum | solution.py:82
  256.0 105.0 %copy-start.1 = (bf16[641,1282]{1,0:T(8,128)(2,1)S(1)}, bf16[641,1282]{1,0:T(8,128)(2,1)}, u32[]{:S(2)}) copy-start(bf16[641,1282]{1,0:T(8,128)(2,1)} %param.9) | copy-start | bytes 4930576
Sparse Core Ops, SparseCore 0:
  227.0 21.2 all-gather.1
  254.9 70.2 all-reduce.3
  327.5 31.7 all-reduce.5
